TPU v7x, 32 devices: a whole 2x2x4 slice. The times are simulated.
32 devices in a mesh: rep: 2 (over x), grp: 8 (over z, y), loc: 2 (over core).
Axes of the slice: x: 2, y: 2, z: 4, core: 2. Of those that a mesh axis runs over, the one named last changes fastest.
Arguments:
- tokens: bfloat16 [4096, 3584], P(('rep', 'grp', 'loc')), parts along dimension 0, may hold values from -6 to 6
- norm_gain: float32 [3584], replicated, may hold values from 0.5 to 1.5
- gate_weight: bfloat16 [8, 3584, 1024], P('grp', 'loc'), may hold values from -0.09375 to 0.09375
- up_weight: bfloat16 [8, 3584, 1024], P('grp', 'loc'), may hold values from -0.09375 to 0.09375
- down_weight: bfloat16 [8, 1024, 3584], P('grp', None, 'loc'), may hold values from -0.1875 to 0.1875
- expert_ids: int32 [4096, 4], P(('rep', 'grp', 'loc')), parts along dimension 0, may hold values from 0 to 7, as said below
- numerators: int32 [4096, 4], P(('rep', 'grp', 'loc')), parts along dimension 0, may hold values from 1 to 128
Outputs:
- moe_out: bfloat16 [4096, 3584], P(('rep', 'grp', 'loc')), parts along dimension 0
There are 2 independent parts, one for each index of `rep`. A program takes and returns all parts, laid end to end along the dimension named above; an argument that names none is the same for every part. Nothing has to cross between parts.
Inputs may be any that keep to these rules, and one draw needn't show every extreme that they name: `expert_ids`: expert e lies in group e // 1. Each token names 4 different experts, one in each of four different groups. In each aligned block of 128 tokens every group is named by exactly half of the tokens, no expert is named by more than 64 tokens, and some expert is named by exactly 64; some experts are named by 64 tokens of every block.
All inputs are finite; a program needn't handle non-finite values.
Results may differ from a plain program's by a relative error of at most 0.015.
Values may be sent and summed in bfloat16 or wider, within the bound.
No kernel may reach another device: no remote copies, remote signals or barrier semaphores. Data moves between devices by JAX's collectives and lax.ppermute only.
A program may use at most 64 MiB of HBM per device.

v0:
```python
import jax
import jax.numpy as jnp
from jax import lax
from jax.sharding import PartitionSpec as P


def local(tokens, norm_gain, gate_weight, up_weight, down_weight, expert_ids, numerators):
    tok_count, width = tokens.shape
    chosen = expert_ids.shape[1]
    experts = lax.axis_size("grp")
    halves = lax.axis_size("loc")
    half_width = width // halves
    capacity = tok_count // 2 - experts // 32 * (23 * tok_count // 64)
    values = tokens.astype(jnp.float32)
    norm_scale = lax.rsqrt(jnp.mean(values * values, axis=-1, keepdims=True) + 1e-06)
    normed = (values * norm_scale * norm_gain).astype(jnp.bfloat16)
    flat_ids = expert_ids.reshape(-1)
    onehot = (flat_ids[:, None] == jnp.arange(experts, dtype=jnp.int32)[None, :]).astype(jnp.int32)
    slot_rank = jnp.sum((jnp.cumsum(onehot, axis=0) - 1) * onehot, axis=1)
    target = (flat_ids * capacity + slot_rank).reshape(tok_count, chosen)
    placed = (
        target[:, :, None] == jnp.arange(experts * capacity, dtype=jnp.int32)[None, None, :]
    ).astype(jnp.float32)
    select = jnp.sum(placed, axis=1).astype(jnp.bfloat16).reshape(tok_count, experts, capacity)
    weights = numerators.astype(jnp.float32) / 128.0
    combine = (
        jnp.sum(placed * weights[:, :, None], axis=1)
        .astype(jnp.bfloat16)
        .reshape(tok_count, experts, capacity)
    )
    feature_halves = normed.reshape(tok_count, halves, half_width)
    outgoing = jnp.einsum(
        "tec,thf->ehcf", select, feature_halves, preferred_element_type=jnp.float32
    ).astype(jnp.bfloat16)
    arrived = lax.all_to_all(
        outgoing.reshape(experts * halves, capacity, half_width),
        ("grp", "loc"),
        split_axis=0,
        concat_axis=0,
        tiled=True,
    )
    expert_input = arrived.reshape(-1, half_width)
    gate_part = jnp.dot(expert_input, gate_weight[0], preferred_element_type=jnp.float32)
    up_part = jnp.dot(expert_input, up_weight[0], preferred_element_type=jnp.float32)
    down_local = down_weight[0]
    gate_sum, up_sum = (
        lax.psum(gate_part.astype(jnp.bfloat16), "loc").astype(jnp.float32),
        lax.psum(up_part.astype(jnp.bfloat16), "loc").astype(jnp.float32),
    )
    hidden_all = (jax.nn.silu(gate_sum) * up_sum).astype(jnp.bfloat16)
    expert_out = jnp.dot(hidden_all, down_local, preferred_element_type=jnp.float32)
    expert_out = expert_out.astype(jnp.bfloat16)
    returned = lax.all_to_all(
        expert_out.reshape(experts * halves, capacity, half_width),
        ("grp", "loc"),
        split_axis=0,
        concat_axis=0,
        tiled=True,
    ).reshape(experts, halves, capacity, half_width)
    mixed = jnp.einsum("tec,ehcf->thf", combine, returned, preferred_element_type=jnp.float32)
    return mixed.reshape(tok_count, width).astype(jnp.bfloat16)


def solution(mesh):
    in_specs = (
        P(("rep", "grp", "loc"), None),
        P(),
        P("grp", "loc", None),
        P("grp", "loc", None),
        P("grp", None, "loc"),
        P(("rep", "grp", "loc"), None),
        P(("rep", "grp", "loc"), None),
    )
    out_specs = P(("rep", "grp", "loc"), None)
    return jax.shard_map(local, mesh=mesh, in_specs=in_specs, out_specs=out_specs, check_vma=False)
```

profile of v0, /device:TPU:13, one launch (start us, length us, event | category | flops | bytes accessed | tf_op | source)
XLA Modules:
  0.0 266.5 jit_solution(13242521310978403542)
XLA Ops:
  6.5 0.8 copy.40
  7.3 0.1 eq.42
  7.4 0.1 eq.38
  7.5 1.4 fusion.20
  9.0 0.7 convert_multiply_fusion.3
  9.7 1.1 reduce-window.6
  10.8 0.2 slice_reduce_fusion
  11.1 0.1 fusion.24
  11.2 0.1 reduce_sum.39
  11.3 0.1 copy.42
  11.4 0.7 multiply_add_fusion
  12.1 0.2 convert_reduce_fusion
  12.3 0.1 copy.44
  12.4 1.5 fusion.22
  13.9 0.2 reshape.66
  14.1 1.1 fusion.11
  15.2 0.4 copy.46
  15.6 0.0 copy-start
  15.6 87.6 %all_to_all.10 = bf16[16,64,1792]{2,1,0:T(8,128)(2,1)S(1)} all-to-all(bf16[16,64,1792]{2,1,0:T(8,128)(2,1)S(1)} %bitcast.44), channel_id=1, replica_groups=mesh['rep'=2,'grp'=8,'loc'=2] {'grp','loc'}, dimensions={0} | all-to-all | bytes 7340032 | tf_op jit(solution)/shard_map/all_to_all | solution.py:35
  103.2 0.0 copy-done
  103.2 5.2 %fusion.17 = bf16[1024,1024]{1,0:T(8,128)(2,1)} fusion(bf16[1024,1792]{1,0:T(8,128)(2,1)S(1)} %bitcast.48, bf16[1,1792,1024]{2,1,0:T(8,128)(2,1)S(1)} %copy-done), kind=kOutput, calls=%fused_computation.22 | convolution fusion | flops 3759144960 | bytes 9437184 | tf_op jit(solution)/shard_map/dot_general | solution.py:44
  108.4 0.0 copy-done.1
  108.4 5.2 %fusion.14 = bf16[1024,1024]{1,0:T(8,128)(2,1)} fusion(bf16[1024,1792]{1,0:T(8,128)(2,1)S(1)} %bitcast.49, bf16[1,1792,1024]{2,1,0:T(8,128)(2,1)S(1)} %copy-done.1), kind=kOutput, calls=%fused_computation.21 | convolution fusion | flops 3759144960 | bytes 9437184 | tf_op jit(solution)/shard_map/dot_general | solution.py:43
  113.6 0.0 all-reduce.3.cloned.1.call-update
  113.6 29.0 %all-reduce.3.cloned.1.call-done = (bf16[1024,1024]{1,0:T(8,128)(2,1)}, bf16[1024,1024]{1,0:T(8,128)(2,1)}) async-done(((bf16[1024,1024]{1,0:T(8,128)(2,1)}, bf16[1024,1024]{1,0:T(8,128)(2,1)}), (bf16[1024,1024]{1,0:T(8,128)(2,1)}, bf16[1024,1024]{1,0:T(8,128)(2,1)})) %all-reduce.3.cloned.1.call-update) | async-done | bytes 4194320 | tf_op jit(solution)/shard_map/psum | solution.py:48
  142.6 9.9 %convolution_convert_fusion.1 = bf16[1024,1792]{1,0:T(8,128)(2,1)} fusion(bf16[1,1024,1792]{2,1,0:T(8,128)(2,1)} %param.11, bf16[1024,1024]{1,0:T(8,128)(2,1)} %get-tuple-element.7, bf16[1024,1024]{1,0:T(8,128)(2,1)} %get-tuple-element.8), kind=kOutput, calls=%fused_computation.10 | convolution fusion | flops 3768320000 | bytes 11534336 | tf_op jit(solution)/shard_map/dot_general | solution.py:51
  152.5 5.9 %all-to-all-start.1 = ((bf16[16,64,1792]{2,1,0:T(8,128)(2,1)}), bf16[16,64,1792]{2,1,0:T(8,128)(2,1)}, u32[]{:S(2)}, u32[]{:S(2)}) async-start(bf16[16,64,1792]{2,1,0:T(8,128)(2,1)} %bitcast.47), calls=%async_computation.1 | async-start | bytes 7340032 | tf_op jit(solution)/shard_map/all_to_all | solution.py:53
  158.3 0.1 copy.43
  158.5 81.1 %all-to-all-done.1 = bf16[16,64,1792]{2,1,0:T(8,128)(2,1)} async-done(((bf16[16,64,1792]{2,1,0:T(8,128)(2,1)}), bf16[16,64,1792]{2,1,0:T(8,128)(2,1)}, u32[]{:S(2)}, u32[]{:S(2)}) %all-to-all-start.1) | async-done | bytes 3670048 | tf_op jit(solution)/shard_map/all_to_all | solution.py:53
  239.6 7.6 %copy.54 = bf16[8,2,64,1792]{3,1,2,0:T(2,128)(2,1)} copy(bf16[8,2,64,1792]{3,2,1,0:T(8,128)(2,1)} %bitcast.13) | data formatting | bytes 7340032 | tf_op jit(solution)/shard_map/reshape | solution.py:59
  247.2 8.8 %dot_general.24 = bf16[3584,64,8]{0,1,2:T(8,128)(2,1)} reshape(bf16[2,1792,64,8]{1,0,2,3:T(2,128)(2,1)} %bitcast.45) | data formatting | bytes 7340032 | tf_op jit(solution)/shard_map/tec,ehcf->thf/dot_general | solution.py:60
  256.1 3.6 %fusion = bf16[128,3584]{1,0:T(8,128)(2,1)} fusion(bf16[128,8,64]{0,2,1:T(8,128)(2,1)S(1)} %bitcast.51, bf16[3584,64,8]{0,1,2:T(8,128)(2,1)} %dot_general.24), kind=kOutput, calls=%fused_computation.3 | convolution fusion | flops 470220800 | bytes 4718592 | tf_op jit(solution)/shard_map/tec,ehcf->thf/dot_general | solution.py:60
  (6 shorter events, 0.1 us)
Async XLA Ops:
  6.5 136.1 %all-reduce.3.cloned.1.call-start = ((), (), s32[]{:S(2)}) async-start(), calls=%async_computation.2 | async-start | bytes 8388608 | tf_op jit(solution)/shard_map/psum | solution.py:48
  15.6 87.6 %copy-start = (bf16[1,1792,1024]{2,1,0:T(8,128)(2,1)S(1)}, bf16[1,1792,1024]{2,1,0:T(8,128)(2,1)}, u32[]{:S(2)}) copy-start(bf16[1,1792,1024]{2,1,0:T(8,128)(2,1)} %param.10) | copy-start | bytes 11010052
  103.2 5.2 %copy-start.1 = (bf16[1,1792,1024]{2,1,0:T(8,128)(2,1)S(1)}, bf16[1,1792,1024]{2,1,0:T(8,128)(2,1)}, u32[]{:S(2)}) copy-start(bf16[1,1792,1024]{2,1,0:T(8,128)(2,1)} %param.9) | copy-start | bytes 11010052
  152.5 87.1 %all-to-all-start.1 = ((bf16[16,64,1792]{2,1,0:T(8,128)(2,1)}), bf16[16,64,1792]{2,1,0:T(8,128)(2,1)}, u32[]{:S(2)}, u32[]{:S(2)}) async-start(bf16[16,64,1792]{2,1,0:T(8,128)(2,1)} %bitcast.47), calls=%async_computation.1 | async-start | bytes 7340032 | tf_op jit(solution)/shard_map/all_to_all | solution.py:53
Sparse Core Ops, SparseCore 0:
  113.7 28.8 all-reduce.2
where the time goes:
time: 267 us
  waiting for transfers between devices  110 us (41%)
  blocking collectives  87.6 us (33%)
  matrix products  25 us (9%)
  local copies, waits for them, and re-layouts  18.7 us (7%)
  between operations  13.5 us (5%)
  starting transfers between devices  5.89 us (2%)
  other arithmetic  5.83 us (2%)
    all_to_all x1, blocking collectives, local(): lax.all_to_all(outgoing.reshape(experts * halves, capacity, half_width),...  87.6 us
    all_to_all x1, waiting for transfers between devices, local(): lax.all_to_all(expert_out.reshape(experts * halves, capacity, half_width)...  81.1 us
    psum x1, waiting for transfers between devices, local(): lax.psum(up_part.astype(jnp.bfloat16), 'loc').astype(jnp.float32)  29 us
    dot_general x1, matrix products, local(): jnp.dot(hidden_all, down_local, preferred_element_type=jnp.float32)  9.86 us
    dot_general x1, local copies, waits for them, and re-layouts, local(): jnp.einsum('tec,ehcf->thf', combine, returned, preferred_element_type=jnp...  8.84 us
    reshape x1, local copies, waits for them, and re-layouts, local(): returned = lax.all_to_all(expert_out.reshape(experts * halves, capacity,...  7.65 us
    all_to_all x1, starting transfers between devices, local(): lax.all_to_all(expert_out.reshape(experts * halves, capacity, half_width)...  5.89 us
  transfers between devices with their start and end apart: 2, of which 2 were waited for; matrix products, arithmetic and copies ran while one was open for 0% of the time, Pallas kernels for 0%

commit v1 on v0

--- a/solution.py
+++ b/solution.py
@@ -45,7 +45,7 @@
     down_local = down_weight[0]
     gate_sum, up_sum = (
         lax.psum(gate_part.astype(jnp.bfloat16), "loc").astype(jnp.float32),
-        lax.psum(up_part.astype(jnp.bfloat16), "loc").astype(jnp.float32),
+        jnp.sum(lax.all_gather(up_part.astype(jnp.bfloat16), "loc"), axis=0).astype(jnp.float32),
     )
     hidden_all = (jax.nn.silu(gate_sum) * up_sum).astype(jnp.bfloat16)
     expert_out = jnp.dot(hidden_all, down_local, preferred_element_type=jnp.float32)

time: 267 us -> 273 us (1.022)
  other arithmetic: 5.83 us -> 9.94 us
  waiting for transfers between devices: 110 us -> 107 us
    psum x1, waiting for transfers between devices: 29 us -> 20.7 us  [local(): lax.psum(gate_part.astype(jnp.bfloat16), 'loc').astype(jnp.float32)]
    all_gather x0 -> x1, waiting for transfers between devices: none -> 5.53 us  [local(): lax.all_gather(up_part.astype(jnp.bfloat16), 'loc')]
    reduce_sum x0 -> x1, other arithmetic: none -> 4.11 us  [local(): jnp.sum(lax.all_gather(up_part.astype(jnp.bfloat16), 'loc'), axis=0)]
    dot_general x1, matrix products: 5.17 us -> 8.53 us  [local(): jnp.dot(expert_input, gate_weight[0], preferred_element_type=jnp.float32)]
  transfers between devices with their start and end apart: 2 -> 3, of which waited for: 2 -> 3; matrix products, arithmetic and copies ran while one was open for 0% -> 5% of each run, Pallas kernels for 0% -> 0%
where the time goes in v1:
time: 273 us
  waiting for transfers between devices  107 us (39%)
  blocking collectives  87.6 us (32%)
  matrix products  27.6 us (10%)
  local copies, waits for them, and re-layouts  20.5 us (8%)
  between operations  13.5 us (5%)
  other arithmetic  9.94 us (4%)
  starting transfers between devices  6.12 us (2%)
    all_to_all x1, blocking collectives, local(): lax.all_to_all(outgoing.reshape(experts * halves, capacity, half_width),...  87.6 us
    all_to_all x1, waiting for transfers between devices, local(): lax.all_to_all(expert_out.reshape(experts * halves, capacity, half_width)...  81.1 us
    psum x1, waiting for transfers between devices, local(): lax.psum(gate_part.astype(jnp.bfloat16), 'loc').astype(jnp.float32)  20.7 us
    dot_general x1, matrix products, local(): jnp.dot(hidden_all, down_local, preferred_element_type=jnp.float32)  9.23 us
    dot_general x1, local copies, waits for them, and re-layouts, local(): jnp.einsum('tec,ehcf->thf', combine, returned, preferred_element_type=jnp...  8.84 us
    dot_general x1, matrix products, local(): jnp.dot(expert_input, gate_weight[0], preferred_element_type=jnp.float32)  8.53 us
    reshape x1, local copies, waits for them, and re-layouts, local(): returned = lax.all_to_all(expert_out.reshape(experts * halves, capacity,...  7.65 us
    all_to_all x1, starting transfers between devices, local(): lax.all_to_all(expert_out.reshape(experts * halves, capacity, half_width)...  5.89 us
  transfers between devices with their start and end apart: 3, of which 3 were waited for; matrix products, arithmetic and copies ran while one was open for 5% of the time, Pallas kernels for 0%

profile of v1, /device:TPU:13, one launch (start us, length us, event | category | flops | bytes accessed | tf_op | source)
XLA Modules:
  0.0 272.6 jit_solution(12138564660163355068)
XLA Ops:
  6.5 0.8 copy.40
  7.3 0.1 eq.42
  7.4 0.1 eq.38
  7.5 1.4 fusion.20
  9.0 0.7 convert_multiply_fusion.3
  9.7 1.1 reduce-window.6
  10.8 0.2 slice_reduce_fusion
  11.1 0.1 fusion.24
  11.2 0.1 reduce_sum.51
  11.3 0.1 copy.42
  11.4 0.7 multiply_add_fusion
  12.1 0.2 convert_reduce_fusion
  12.3 0.1 copy.44
  12.4 1.5 fusion.22
  13.9 0.2 reshape.66
  14.1 1.1 fusion.11
  15.2 0.4 copy.46
  15.6 87.6 %all_to_all.10 = bf16[16,64,1792]{2,1,0:T(8,128)(2,1)S(1)} all-to-all(bf16[16,64,1792]{2,1,0:T(8,128)(2,1)S(1)} %bitcast.45), channel_id=1, replica_groups=mesh['rep'=2,'grp'=8,'loc'=2] {'grp','loc'}, dimensions={0} | all-to-all | bytes 7340032 | tf_op jit(solution)/shard_map/all_to_all | solution.py:35
  103.2 1.8 copy-done
  105.0 5.2 %fusion.17 = bf16[1024,1024]{1,0:T(8,128)(2,1)} fusion(bf16[1024,1792]{1,0:T(8,128)(2,1)S(1)} %bitcast.49, bf16[1,1792,1024]{2,1,0:T(8,128)(2,1)S(1)} %copy-done.1), kind=kOutput, calls=%fused_computation.22 | convolution fusion | flops 3759144960 | bytes 9437184 | tf_op jit(solution)/shard_map/dot_general | solution.py:44
  110.2 0.2 all-reduce.2.cloned.1.call-start
  110.4 8.5 %fusion.14 = bf16[1024,1024]{1,0:T(8,128)(2,1)} fusion(bf16[1024,1792]{1,0:T(8,128)(2,1)} %bitcast.50, bf16[1,1792,1024]{2,1,0:T(8,128)(2,1)} %param.9), kind=kOutput, calls=%fused_computation.21 | convolution fusion | flops 3759144960 | bytes 9437184 | tf_op jit(solution)/shard_map/dot_general | solution.py:43
  119.0 5.5 %all-gather.3.cloned.1.call-done = bf16[2048,1024]{1,0:T(8,128)(2,1)} async-done(((bf16[1024,1024]{1,0:T(8,128)(2,1)}), bf16[2048,1024]{1,0:T(8,128)(2,1)}) %all-gather.3.cloned.1.call-update) | async-done | bytes 4194320 | tf_op jit(solution)/shard_map/all_gather | solution.py:48
  124.5 4.1 %reduce_sum.55 = bf16[1024,1024]{1,0:T(8,128)(2,1)S(1)} reduce(bf16[2,1024,1024]{2,1,0:T(8,128)(2,1)} %bitcast.48, bf16[]{:T(256)} %constant.26.clone.1), dimensions={0}, to_apply=%region_7.8 | reduce | flops 1048576 | bytes 6291458 | tf_op jit(solution)/shard_map/reduce_sum | solution.py:48
  128.6 20.7 %all-reduce.2.cloned.1.call-done = bf16[1024,1024]{1,0:T(8,128)(2,1)} async-done(((bf16[1024,1024]{1,0:T(8,128)(2,1)}), bf16[1024,1024]{1,0:T(8,128)(2,1)}) %all-reduce.2.cloned.1.call-update) | async-done | bytes 2097168 | tf_op jit(solution)/shard_map/psum | solution.py:47
  149.3 9.2 %convolution_convert_fusion.1 = bf16[1024,1792]{1,0:T(8,128)(2,1)} fusion(bf16[1,1024,1792]{2,1,0:T(8,128)(2,1)} %param.11, bf16[1024,1024]{1,0:T(8,128)(2,1)S(1)} %reduce_sum.55, bf16[1024,1024]{1,0:T(8,128)(2,1)} %all-reduce.2.cloned.1.call-done), kind=kOutput, calls=%fused_computation.10 | convolution fusion | flops 3768320000 | bytes 11534336 | tf_op jit(solution)/shard_map/dot_general | solution.py:51
  158.6 5.9 %all-to-all-start.1 = ((bf16[16,64,1792]{2,1,0:T(8,128)(2,1)}), bf16[16,64,1792]{2,1,0:T(8,128)(2,1)}, u32[]{:S(2)}, u32[]{:S(2)}) async-start(bf16[16,64,1792]{2,1,0:T(8,128)(2,1)} %bitcast.51), calls=%async_computation.1 | async-start | bytes 7340032 | tf_op jit(solution)/shard_map/all_to_all | solution.py:53
  164.4 0.1 copy.43
  164.6 81.1 %all-to-all-done.1 = bf16[16,64,1792]{2,1,0:T(8,128)(2,1)} async-done(((bf16[16,64,1792]{2,1,0:T(8,128)(2,1)}), bf16[16,64,1792]{2,1,0:T(8,128)(2,1)}, u32[]{:S(2)}, u32[]{:S(2)}) %all-to-all-start.1) | async-done | bytes 3670048 | tf_op jit(solution)/shard_map/all_to_all | solution.py:53
  245.7 7.6 %copy.54 = bf16[8,2,64,1792]{3,1,2,0:T(2,128)(2,1)} copy(bf16[8,2,64,1792]{3,2,1,0:T(8,128)(2,1)} %bitcast.14) | data formatting | bytes 7340032 | tf_op jit(solution)/shard_map/reshape | solution.py:59
  253.3 8.8 %dot_general.24 = bf16[3584,64,8]{0,1,2:T(8,128)(2,1)} reshape(bf16[2,1792,64,8]{1,0,2,3:T(2,128)(2,1)} %bitcast.46) | data formatting | bytes 7340032 | tf_op jit(solution)/shard_map/tec,ehcf->thf/dot_general | solution.py:60
  262.2 3.6 %fusion = bf16[128,3584]{1,0:T(8,128)(2,1)} fusion(bf16[128,8,64]{0,2,1:T(8,128)(2,1)S(1)} %bitcast.53, bf16[3584,64,8]{0,1,2:T(8,128)(2,1)} %dot_general.24), kind=kOutput, calls=%fused_computation.3 | convolution fusion | flops 470220800 | bytes 4718592 | tf_op jit(solution)/shard_map/tec,ehcf->thf/dot_general | solution.py:60
  (10 shorter events, 0.1 us)
Async XLA Ops:
  6.5 118.0 %all-gather.3.cloned.1.call-start = ((), (), s32[]{:S(2)}) async-start(), calls=%async_computation.3 | async-start | bytes 6291456 | tf_op jit(solution)/shard_map/all_gather | solution.py:48
  15.6 89.4 %copy-start.1 = (bf16[1,1792,1024]{2,1,0:T(8,128)(2,1)S(1)}, bf16[1,1792,1024]{2,1,0:T(8,128)(2,1)}, u32[]{:S(2)}) copy-start(bf16[1,1792,1024]{2,1,0:T(8,128)(2,1)} %param.10) | copy-start | bytes 11010052
  103.2 1.8 copy-start
  110.2 39.2 %all-reduce.2.cloned.1.call-start = ((), (), s32[]{:S(2)}) async-start(), calls=%async_computation.2 | async-start | bytes 4194304 | tf_op jit(solution)/shard_map/psum | solution.py:47
  158.6 87.1 %all-to-all-start.1 = ((bf16[16,64,1792]{2,1,0:T(8,128)(2,1)}), bf16[16,64,1792]{2,1,0:T(8,128)(2,1)}, u32[]{:S(2)}, u32[]{:S(2)}) async-start(bf16[16,64,1792]{2,1,0:T(8,128)(2,1)} %bitcast.51), calls=%async_computation.1 | async-start | bytes 7340032 | tf_op jit(solution)/shard_map/all_to_all | solution.py:53
Sparse Core Ops, SparseCore 0:
  110.3 14.1 all-gather.2
  126.8 22.4 all-reduce.1
